TPU v7x, 128 devices: a whole 4x4x4 slice. The times are simulated.
128 devices in a mesh: grp: 4 (over y), in: 32 (over z, x, core).
Axes of the slice: x: 4, y: 4, z: 4, core: 2. Of those that a mesh axis runs over, the one named last changes fastest.
Arguments:
- unfolding: float32 [1024, 524288], P(None, ('grp', 'in')), may hold values from -300 to 300
- start_basis: float32 [1024, 128], replicated, may hold values from -6 to 6
Outputs:
- factor: float32 [1024, 128], replicated
- core_block: float32 [128, 524288], P(None, ('grp', 'in'))
All inputs are finite; a program needn't handle non-finite values.
Results may differ from a plain program's by a relative error of at most 0.0003.
Values sent between devices are 32-bit elements; how exact they have to be, the bound alone decides.
A program may use at most 128 MiB of HBM per device.

v0:
```python
import jax
import jax.numpy as jnp
from jax import lax
from jax.sharding import PartitionSpec as P

ITERS = 3


def orthonormal_rows(image, inner):
    lower = jnp.linalg.cholesky(inner)
    return lax.linalg.triangular_solve(lower, image, left_side=False, lower=True, transpose_a=True)


def per_device(unfolding, start_basis):
    basis = start_basis
    slab = lax.psum_scatter(
        lax.dot_general(
            unfolding,
            unfolding,
            (((1,), (1,)), ((), ())),
            precision=lax.Precision.HIGHEST,
            preferred_element_type=jnp.float32,
        ),
        "in",
        scatter_dimension=0,
        tiled=True,
    )
    slab = lax.psum(slab, "grp")
    gram = lax.all_gather(slab, "in", axis=0, tiled=True)
    for step in range(ITERS):
        image = jnp.dot(
            gram, basis, precision=lax.Precision.HIGHEST, preferred_element_type=jnp.float32
        )
        inner = jnp.dot(
            image.T, image, precision=lax.Precision.HIGHEST, preferred_element_type=jnp.float32
        )
        basis = orthonormal_rows(image, inner)
    core_block = lax.dot_general(
        basis,
        unfolding,
        (((0,), (0,)), ((), ())),
        precision=lax.Precision.HIGHEST,
        preferred_element_type=jnp.float32,
    )
    return (basis, core_block)


def solution(mesh):
    in_specs = (P(None, ("grp", "in")), P())
    out_specs = (P(), P(None, ("grp", "in")))
    return jax.shard_map(
        per_device, mesh=mesh, in_specs=in_specs, out_specs=out_specs, check_vma=False
    )
```

profile of v0, /device:TPU:1, one launch (start us, length us, event | category | flops | bytes accessed | tf_op | source)
XLA Modules:
  0.0 355.9 jit_solution(5176587068454633123)
XLA Ops:
  7.2 59.5 %fusion.13 = f32[1024,1024]{1,0:T(8,128)} fusion(f32[1024,4096]{1,0:T(8,128)} %param.5), kind=kOutput, calls=%fused_computation.28 | convolution fusion | flops 51539607552 | bytes 20971520 | tf_op jit(solution)/shard_map/dot_general | solution.py:17
  66.8 84.1 %reduce-scatter.2.cloned.1.call-done = f32[32,1024]{1,0:T(8,128)} async-done(((f32[1024,1024]{1,0:T(8,128)}), f32[32,1024]{1,0:T(8,128)}) %reduce-scatter.2.cloned.1.call-update) | async-done | bytes 131088 | tf_op jit(solution)/shard_map/reduce_scatter | solution.py:16
  151.2 42.4 %all-reduce.2.cloned.1.call-done = f32[32,1024]{1,0:T(8,128)} async-done(((f32[32,1024]{1,0:T(8,128)}), f32[32,1024]{1,0:T(8,128)}) %all-reduce.2.cloned.1.call-update) | async-done | bytes 131088 | tf_op jit(solution)/shard_map/psum | solution.py:28
  193.7 51.3 %all-gather.2.cloned.1.call-done = f32[1024,1024]{1,0:T(8,128)} async-done(((f32[32,1024]{1,0:T(8,128)}), f32[1024,1024]{1,0:T(8,128)}) %all-gather.2.cloned.1.call-update) | async-done | bytes 4194320 | tf_op jit(solution)/shard_map/all_gather | solution.py:29
  245.0 5.2 %fusion.14 = f32[1024,128]{1,0:T(8,128)S(1)} fusion(f32[1024,1024]{1,0:T(8,128)} %all-gather.2.cloned.1.call-done, f32[1024,128]{1,0:T(8,128)S(1)} %copy-done), kind=kOutput, calls=%fused_computation.29 | convolution fusion | flops 1610612736 | bytes 5242880 | tf_op jit(solution)/shard_map/dot_general | solution.py:31
  250.2 1.0 fusion.15
  251.3 11.7 %cholesky.59 = f32[128,128]{1,0:T(8,128)S(1)} custom-call(f32[128,128]{1,0:T(8,128)S(1)} %fusion.8), custom_call_target="Cholesky" | custom-call | tf_op jit(solution)/shard_map/jit(cholesky)/cholesky | solution.py:10
  263.1 0.6 compare_reduce_fusion.2
  263.7 0.7 fusion
  264.4 9.8 %custom-call.7 = f32[1,128,128]{1,2,0:T(8,128)S(1)} custom-call(f32[1,128,128]{2,1,0:T(8,128)S(1)} %fusion), custom_call_target="InvertDiagBlocksLowerTriangular" | custom-call | tf_op jit(solution)/shard_map/triangular_solve/custom-call.0 | solution.py:11
  274.9 5.4 %fusion.16 = f32[1024,128]{1,0:T(8,128)S(1)} fusion(f32[1024,1024]{1,0:T(8,128)} %all-gather.2.cloned.1.call-done, f32[1024,128]{0,1:T(8,128)S(1)} %convolution_bitcast_fusion.2), kind=kOutput, calls=%fused_computation.31 | convolution fusion | flops 1610612736 | bytes 5242880 | tf_op jit(solution)/shard_map/dot_general | solution.py:31
  280.3 1.0 fusion.17
  281.4 11.7 %cholesky.70 = f32[128,128]{1,0:T(8,128)S(1)} custom-call(f32[128,128]{1,0:T(8,128)S(1)} %fusion.6), custom_call_target="Cholesky" | custom-call | tf_op jit(solution)/shard_map/jit(cholesky)/cholesky | solution.py:10
  293.2 0.6 compare_reduce_fusion.1
  293.8 0.7 fusion.1
  294.5 9.8 %custom-call.8 = f32[1,128,128]{1,2,0:T(8,128)S(1)} custom-call(f32[1,128,128]{2,1,0:T(8,128)S(1)} %fusion.1), custom_call_target="InvertDiagBlocksLowerTriangular" | custom-call | tf_op jit(solution)/shard_map/triangular_solve/custom-call.0 | solution.py:11
  304.9 5.5 %fusion.18 = f32[1024,128]{1,0:T(8,128)S(1)} fusion(f32[1024,1024]{1,0:T(8,128)} %all-gather.2.cloned.1.call-done, f32[1024,128]{0,1:T(8,128)S(1)} %convolution_bitcast_fusion.1), kind=kOutput, calls=%fused_computation.33 | convolution fusion | flops 1610612736 | bytes 5242880 | tf_op jit(solution)/shard_map/dot_general | solution.py:31
  310.4 1.0 fusion.19
  311.6 11.7 %cholesky.81 = f32[128,128]{1,0:T(8,128)S(1)} custom-call(f32[128,128]{1,0:T(8,128)S(1)} %fusion.4), custom_call_target="Cholesky" | custom-call | tf_op jit(solution)/shard_map/jit(cholesky)/cholesky | solution.py:10
  324.0 0.7 fusion.2
  324.6 9.8 %custom-call.9 = f32[1,128,128]{1,2,0:T(8,128)S(1)} custom-call(f32[1,128,128]{2,1,0:T(8,128)S(1)} %fusion.2), custom_call_target="InvertDiagBlocksLowerTriangular" | custom-call | tf_op jit(solution)/shard_map/triangular_solve/custom-call.0 | solution.py:11
  334.4 0.6 convolution_bitcast_fusion
  335.1 1.0 copy.7
  336.1 12.9 %fusion.20 = f32[128,4096]{1,0:T(8,128)} fusion(f32[1024,128]{0,1:T(8,128)S(1)} %convolution_bitcast_fusion, f32[1024,4096]{1,0:T(8,128)} %param.5), kind=kOutput, calls=%fused_computation.35 | convolution fusion | flops 6442450944 | bytes 19398656 | tf_op jit(solution)/shard_map/dot_general | solution.py:38
  (20 shorter events, 2.7 us)
Async XLA Ops:
  7.2 237.8 %copy-start = (f32[1024,128]{1,0:T(8,128)S(1)}, f32[1024,128]{1,0:T(8,128)}, u32[]{:S(2)}) copy-start(f32[1024,128]{1,0:T(8,128)} %param.6) | copy-start | bytes 1572868
  7.2 143.8 %reduce-scatter.2.cloned.1.call-start = ((), (), s32[]{:S(2)}) async-start(), calls=%async_computation.1 | async-start | bytes 4325376 | tf_op jit(solution)/shard_map/reduce_scatter | solution.py:16
  66.8 126.8 %all-reduce.2.cloned.1.call-start = ((), (), s32[]{:S(2)}) async-start(), calls=%async_computation.2 | async-start | bytes 262144 | tf_op jit(solution)/shard_map/psum | solution.py:28
  151.0 94.0 %all-gather.2.cloned.1.call-start = ((), (), s32[]{:S(2)}) async-start(), calls=%async_computation.3 | async-start | bytes 4325376 | tf_op jit(solution)/shard_map/all_gather | solution.py:29
Sparse Core Ops, SparseCore 0:
  66.9 84.0 reduce-scatter.1
  153.3 40.3 all-reduce.1
  195.9 49.0 all-gather.1
where the time goes:
time: 361 us; the launch traced here: 356 us
  waiting for transfers between devices  178 us (49%)
  matrix products  93.5 us (26%)
  other arithmetic  68.6 us (19%)
  between operations  14.3 us (4%)
    reduce_scatter x1, waiting for transfers between devices, per_device(): lax.psum_scatter(lax.dot_general(unfolding, unfolding, (((1,), (1,)), (()...  84.1 us
    dot_general x1, matrix products, per_device(): lax.dot_general(unfolding, unfolding, (((1,), (1,)), ((), ())), precision...  59.5 us
    all_gather x1, waiting for transfers between devices, per_device(): gram = lax.all_gather(slab, 'in', axis=0, tiled=True)  51.3 us
    psum x1, waiting for transfers between devices, per_device(): slab = lax.psum(slab, 'grp')  42.4 us
    another operation x9, other arithmetic, orthonormal_rows(): lower = jnp.linalg.cholesky(inner)  37.2 us
    another operation x6, other arithmetic, orthonormal_rows(): lax.linalg.triangular_solve(lower, image, left_side=False, lower=True, tr...  31.4 us
    dot_general x3, matrix products, per_device(): jnp.dot(gram, basis, precision=lax.Precision.HIGHEST, preferred_element_t...  16.1 us
    dot_general x1, matrix products, per_device(): lax.dot_general(basis, unfolding, (((0,), (0,)), ((), ())), precision=lax...  12.9 us
  transfers between devices with their start and end apart: 3, of which 3 were waited for; matrix products, arithmetic and copies ran while one was open for 0% of the time, Pallas kernels for 0%

commit v1 on v0

v1 whole, which is shorter than its diff:
```python
import functools

import jax
import jax.numpy as jnp
from jax import lax
from jax.experimental import pallas as pl
from jax.experimental.pallas import tpu as pltpu
from jax.sharding import PartitionSpec as P

HI = lax.Precision.HIGHEST
F32 = jnp.float32
BF = jnp.bfloat16

def split(x):
    hi = x.astype(BF)
    return hi, (x - hi.astype(F32)).astype(BF)

def dg(a, b, ca, cb):
    return lax.dot_general(a, b, (((ca,), (cb,)), ((), ())), preferred_element_type=F32)

def eliminate(a_ref, q_ref, w_ref):
    sub = lax.broadcasted_iota(jnp.int32, (8, 128), 0)
    lane = lax.broadcasted_iota(jnp.int32, (8, 128), 1)
    M = [a_ref[8*p:8*p+8, :] for p in range(16)]
    Q = [jnp.where(lane == sub + 8*p, 1.0, 0.0).astype(F32) for p in range(16)]
    for p in range(16):
        P, R = M[p], Q[p]
        cols = [jnp.broadcast_to(P[:, 8*p+c:8*p+c+1], (8, 128)) for c in range(8)]
        piv = []
        recs = []
        for r in range(8):
            d = jnp.broadcast_to(cols[r][r:r+1, :], (8, 128))
            rec = 1.0 / d
            piv.append(d); recs.append(rec)
            if r == 7: break
            m = jnp.where(sub > r, cols[r] * rec, 0.0)
            for c in range(r+1, 8):
                cols[c] = cols[c] - m * jnp.broadcast_to(cols[c][r:r+1, :], (8, 128))
            P = P - m * jnp.broadcast_to(P[r:r+1, :], (8, 128))
            R = R - m * jnp.broadcast_to(R[r:r+1, :], (8, 128))
        dv = piv[7]; rv = recs[7]
        for r in range(7):
            dv = jnp.where(sub == r, piv[r], dv)
            rv = jnp.where(sub == r, recs[r], rv)
        w_ref[8*p:8*p+8, :] = R * (1.0 / jnp.sqrt(dv))
        if p < 15:
            T = jnp.transpose(P * rv)
            pr = [jnp.broadcast_to(P[r:r+1, :], (8, 128)) for r in range(8)]
            qr = [jnp.broadcast_to(R[r:r+1, :], (8, 128)) for r in range(8)]
            for i in range(p+1, 16):
                for r in range(8):
                    mm = jnp.broadcast_to(T[8*i:8*i+8, r:r+1], (8, 128))
                    M[i] = M[i] - mm * pr[r]
                    Q[i] = Q[i] - mm * qr[r]

def k2_kernel(x_ref, s_ref, f_ref, ghi, glo, img, a_ref, q_ref, w_ref, *, iters=3):
    k = 0
    for i in range(4):
        for j in range(i, 4):
            blk = jnp.concatenate([x_ref[k, :256, :], x_ref[k, 256:, :]], axis=1)
            if i == j:
                blk = 0.5 * (blk + blk.T)
            hi, lo = split(blk)
            ghi[256*i:256*i+256, 256*j:256*j+256] = hi
            glo[256*i:256*i+256, 256*j:256*j+256] = lo
            if i != j:
                ghi[256*j:256*j+256, 256*i:256*i+256] = hi.T
                glo[256*j:256*j+256, 256*i:256*i+256] = lo.T
            k += 1
    f_ref[...] = s_ref[...]
    def body(t, _):
        bh, bl = split(f_ref[...])
        b2 = jnp.concatenate([bh, bl], axis=1)
        for i in range(4):
            r2 = dg(ghi[256*i:256*i+256, :], b2, 1, 0)
            r1 = dg(glo[256*i:256*i+256, :], bh, 1, 0)
            img[256*i:256*i+256, :] = r2[:, :128] + (r2[:, 128:] + r1)
        im = img[...]
        a_ref[...] = lax.dot_general(im, im, (((0,), (0,)), ((), ())), precision=HI, preferred_element_type=F32)
        eliminate(a_ref, q_ref, w_ref)
        f_ref[...] = lax.dot_general(img[...], w_ref[...], (((1,), (1,)), ((), ())), precision=HI, preferred_element_type=F32)
        return 0
    lax.fori_loop(0, iters, body, 0)

def k2(x, s, iters=3):
    v = pl.BlockSpec(memory_space=pltpu.VMEM)
    return pl.pallas_call(functools.partial(k2_kernel, iters=iters), out_shape=jax.ShapeDtypeStruct((1024, 128), F32),
        in_specs=[v, v], out_specs=v,
        scratch_shapes=[pltpu.VMEM((1024,1024),BF), pltpu.VMEM((1024,1024),BF), pltpu.VMEM((1024,128),F32),
                        pltpu.VMEM((128,128),F32), pltpu.VMEM((128,128),F32), pltpu.VMEM((128,128),F32)],
        compiler_params=pltpu.CompilerParams(vmem_limit_bytes=60<<20))(x, s)

def gram_kernel(u_ref, o_ref, h_ref, l_ref):
    t = pl.program_id(0)
    h, l = split(u_ref[...])
    h_ref[...] = h; l_ref[...] = l
    @pl.when(t == 0)
    def _(): o_ref[...] = jnp.zeros_like(o_ref)
    k = 0
    for i in range(4):
        for j in range(i, 4):
            hi, hj = h_ref[256*i:256*i+256, :], h_ref[256*j:256*j+256, :]
            li, lj = l_ref[256*i:256*i+256, :], l_ref[256*j:256*j+256, :]
            r = dg(hi, hj, 1, 1)
            if i == j:
                r = r + 2.0 * dg(hi, lj, 1, 1)
            else:
                r = r + (dg(hi, lj, 1, 1) + dg(li, hj, 1, 1))
            o_ref[k, :256, :] += r[:, :128]
            o_ref[k, 256:, :] += r[:, 128:]
            k += 1

def gram(u, tk=512):
    return pl.pallas_call(gram_kernel, out_shape=jax.ShapeDtypeStruct((10, 512, 128), F32),
        grid=(u.shape[1]//tk,),
        in_specs=[pl.BlockSpec((1024, tk), lambda t: (0, t))],
        out_specs=pl.BlockSpec((10, 512, 128), lambda t: (0, 0, 0)),
        scratch_shapes=[pltpu.VMEM((1024, tk), BF), pltpu.VMEM((1024, tk), BF)],
        compiler_params=pltpu.CompilerParams(vmem_limit_bytes=60<<20, dimension_semantics=("arbitrary",)))(u)

def core_kernel(f_ref, u_ref, o_ref, f2_ref):
    @pl.when(pl.program_id(0) == 0)
    def _():
        ft = f_ref[...].T
        fh, fl = split(ft)
        f2_ref[:128, :] = fh; f2_ref[128:, :] = fl
    h, l = split(u_ref[...])
    r = dg(f2_ref[...], h, 1, 0)
    o_ref[...] = r[:128, :] + (r[128:, :] + dg(f2_ref[:128, :], l, 1, 0))

def core(f, u, tk=512):
    return pl.pallas_call(core_kernel, out_shape=jax.ShapeDtypeStruct((128, u.shape[1]), F32),
        grid=(u.shape[1]//tk,),
        in_specs=[pl.BlockSpec((1024, 128), lambda t: (0, 0)), pl.BlockSpec((1024, tk), lambda t: (0, t))],
        out_specs=pl.BlockSpec((128, tk), lambda t: (0, t)),
        scratch_shapes=[pltpu.VMEM((256, 1024), BF)],
        compiler_params=pltpu.CompilerParams(vmem_limit_bytes=60<<20, dimension_semantics=("arbitrary",)))(f, u)
F32 = jnp.float32
STAGES = 5
MESH = pl.DeviceIdType.MESH

class Net:
    def __init__(self):
        self.y = lax.axis_index("grp")
        inn = lax.axis_index("in")
        self.core = lax.rem(inn, 2)
        self.x = lax.rem(inn // 2, 4)
        self.z = inn // 8
    def coord(self, axis):
        return (self.x, self.y, self.z)[axis]
    def step(self, axis, d):
        return lax.rem(self.coord(axis) + d, 4)
    def peer(self, axis, d):
        c = [self.x, self.y, self.z]
        c[axis] = self.step(axis, d)
        return (c[1], (c[2] * 4 + c[0]) * 2 + self.core)
    def twin(self):
        return (self.y, (self.z * 4 + self.x) * 2 + 1 - self.core)
    def barrier(self):
        b = pltpu.get_barrier_semaphore()
        pl.semaphore_signal(b, inc=1, device_id=self.twin(), device_id_type=MESH)
        for a in range(3):
            for d in (1, 2, 3):
                pl.semaphore_signal(b, inc=1, device_id=self.peer(a, d), device_id_type=MESH)
        pl.semaphore_wait(b, 10)

def ar_kernel(x_ref, o_ref, b0, b1, b2, b3, a0, a1, a2, ssem, rsem):
    net = Net()
    net.barrier()
    def rc(src, dst, s, k, dev):
        c = pltpu.make_async_remote_copy(src_ref=src, dst_ref=dst, send_sem=ssem.at[s, k], recv_sem=rsem.at[s, k], device_id=dev, device_id_type=MESH)
        c.start()
        return c
    sent = []
    order = [[(s + l) % 3 for l in range(3)] for s in range(STAGES)]
    m = pl.multiple_of
    cps = []
    for s in range(STAGES):
        cps.append([rc(x_ref.at[2 * s + 1 - net.core], b0.at[s], s, 0, net.twin())])
    rows = (512, 128, 32, 8)
    bufs = (b1, b2, b3)
    accs = (a0, a1, a2)
    for lvl in range(3):
        n = rows[lvl + 1]
        nxt = []
        for s in range(STAGES):
            for c in cps[s]:
                c.wait_recv()
            sent += cps[s]
            acc = accs[lvl].at[s]
            if lvl == 0:
                acc[...] = x_ref[2 * s + net.core] + b0[s]
            else:
                p = net.coord(order[s][lvl - 1])
                v = accs[lvl - 1][s, pl.ds(m(p * rows[lvl], rows[lvl]), rows[lvl]), :]
                acc[...] = v + (bufs[lvl - 1][s, 0] + (bufs[lvl - 1][s, 1] + bufs[lvl - 1][s, 2]))
            ax = order[s][lvl]
            cur = []
            for d in (1, 2, 3):
                q = net.step(ax, d)
                cur.append(rc(acc.at[pl.ds(m(q * n, n), n), :], bufs[lvl].at[s, d - 1], s, 3 * lvl + d, net.peer(ax, d)))
            nxt.append(cur)
        cps = nxt
    offs = []
    for s in range(STAGES):
        c1, c2, c3 = (net.coord(a) for a in order[s])
        offs.append((c1 * 128, c1 * 128 + c2 * 32, c1 * 128 + c2 * 32 + c3 * 8))
    for lvl in (2, 1, 0):
        n = rows[lvl + 1]
        nxt = []
        for s in range(STAGES):
            for c in cps[s]:
                c.wait_recv()
            sent += cps[s]
            unit = 2 * s + net.core
            ax = order[s][lvl]
            here = o_ref.at[unit, pl.ds(m(offs[s][lvl], n), n), :]
            if lvl == 2:
                p = net.coord(ax)
                v = a2[s, pl.ds(m(p * 8, 8), 8), :]
                here[...] = v + (b3[s, 0] + (b3[s, 1] + b3[s, 2]))
            nxt.append([rc(here, here, s, 9 + 3 * lvl + d, net.peer(ax, d)) for d in (1, 2, 3)])
        cps = nxt
    nxt = []
    for s in range(STAGES):
        for c in cps[s]:
            c.wait_recv()
        sent += cps[s]
        unit = 2 * s + net.core
        nxt.append(rc(o_ref.at[unit], o_ref.at[unit], s, 19, net.twin()))
    for c in nxt:
        c.wait_recv()
    for c in sent + nxt:
        c.wait_send()

def allreduce(x):
    v = pl.BlockSpec(memory_space=pltpu.VMEM)
    S = STAGES
    return pl.pallas_call(ar_kernel, out_shape=jax.ShapeDtypeStruct((10, 512, 128), F32),
        in_specs=[v], out_specs=v,
        scratch_shapes=[pltpu.VMEM((S, 512, 128), F32), pltpu.VMEM((S, 3, 128, 128), F32), pltpu.VMEM((S, 3, 32, 128), F32), pltpu.VMEM((S, 3, 8, 128), F32),
                        pltpu.VMEM((S, 512, 128), F32), pltpu.VMEM((S, 128, 128), F32), pltpu.VMEM((S, 32, 128), F32),
                        pltpu.SemaphoreType.DMA((S, 20)), pltpu.SemaphoreType.DMA((S, 20))],
        compiler_params=pltpu.CompilerParams(vmem_limit_bytes=60<<20, collective_id=0, has_side_effects=True))(x)


def per_device(unfolding, start_basis):
    packed = allreduce(gram(unfolding))
    factor = k2(packed, start_basis)
    return factor, core(factor, unfolding, 1024)


def solution(mesh):
    in_specs = (P(None, ("grp", "in")), P())
    out_specs = (P(), P(None, ("grp", "in")))
    return jax.shard_map(
        per_device, mesh=mesh, in_specs=in_specs, out_specs=out_specs, check_vma=False
    )
```

time: 361 us -> 102 us (0.28); the launches traced: 356 us -> 102 us
  waiting for transfers between devices: 178 us -> 0 us
  Pallas kernels: 0 us -> 102 us
  matrix products: 93.5 us -> 0 us
  other arithmetic: 68.6 us -> 0 us
  between operations: 14.3 us -> 0.64 us
    pallas_call x0 -> x4, Pallas kernels: none -> 102 us  [the longest x1 43.1 us: allreduce(): pl.pallas_call(ar_kernel, out_shape=jax.ShapeDtypeStruct((10, 512, 128),...]
    dot_general x8 -> x0, matrix products: 91.6 us -> none  [the longest x1 59.5 us: per_device(): lax.dot_general(unfolding, unfolding, (((1,), (1,)), ((), ())), precision...]
    reduce_scatter x1 -> x0, waiting for transfers between devices: 84.1 us -> none  [per_device(): lax.psum_scatter(lax.dot_general(unfolding, unfolding, (((1,), (1,)), (()...]
    another operation x15 -> x0, other arithmetic: 68.6 us -> none  [the longest x9 37.2 us: orthonormal_rows(): lower = jnp.linalg.cholesky(inner)]
    all_gather x1 -> x0, waiting for transfers between devices: 51.3 us -> none  [per_device(): gram = lax.all_gather(slab, 'in', axis=0, tiled=True)]
    psum x1 -> x0, waiting for transfers between devices: 42.4 us -> none  [per_device(): slab = lax.psum(slab, 'grp')]
  transfers between devices with their start and end apart: 3 -> 0, of which waited for: 3 -> 0; matrix products, arithmetic and copies ran while one was open for 0% -> 0% of each run, Pallas kernels for 0% -> 0%
where the time goes in v1:
time: 102 us
  Pallas kernels  102 us (100%)
    pallas_call x1, Pallas kernels, allreduce(): pl.pallas_call(ar_kernel, out_shape=jax.ShapeDtypeStruct((10, 512, 128),...  43.1 us
    pallas_call x1, Pallas kernels, k2(): pl.pallas_call(functools.partial(k2_kernel, iters=iters), out_shape=jax.S...  27.6 us
    pallas_call x1, Pallas kernels, gram(): pl.pallas_call(gram_kernel, out_shape=jax.ShapeDtypeStruct((10, 512, 128)...  21.4 us
    pallas_call x1, Pallas kernels, core(): pl.pallas_call(core_kernel, out_shape=jax.ShapeDtypeStruct((128, u.shape[...  9.46 us

profile of v1, /device:TPU:1, one launch (start us, length us, event | category | flops | bytes accessed | tf_op | source)
XLA Modules:
  0.0 102.3 jit_solution(7747310911612704165)
XLA Ops:
  0.6 21.4 %shard_map.41.x_ref = f32[10,512,128]{2,1,0:T(8,128)} custom-call(f32[1024,4096]{1,0:T(8,128)} %u_ref.3), custom_call_target="tpu_custom_call" | custom-call | tf_op jit(solution)/shard_map/pallas_call | solution.py:114
  22.1 43.1 %shard_map.42.x_ref = f32[10,512,128]{2,1,0:T(8,128)} custom-call(f32[10,512,128]{2,1,0:T(8,128)} %shard_map.41.x_ref), custom_call_target="tpu_custom_call" | custom-call | tf_op jit(solution)/shard_map/pallas_call | solution.py:239
  65.2 27.6 %shard_map.43.f_ref = f32[1024,128]{1,0:T(8,128)} custom-call(f32[10,512,128]{2,1,0:T(8,128)} %shard_map.42.x_ref, f32[1024,128]{1,0:T(8,128)} %s_ref.1), custom_call_target="tpu_custom_call" | custom-call | tf_op jit(solution)/shard_map/pallas_call | solution.py:87
  92.8 9.5 %shard_map.44 = f32[128,4096]{1,0:T(8,128)} custom-call(f32[1024,128]{1,0:T(8,128)} %shard_map.43.f_ref, f32[1024,4096]{1,0:T(8,128)} %u_ref.3), custom_call_target="tpu_custom_call" | custom-call | tf_op jit(solution)/shard_map/pallas_call | solution.py:132

commit v2 on v1

--- a/solution.py
+++ b/solution.py
@@ -55,8 +55,8 @@
 
 def k2_kernel(x_ref, s_ref, f_ref, ghi, glo, img, a_ref, q_ref, w_ref, *, iters=3):
     k = 0
-    for i in range(4):
-        for j in range(i, 4):
+    for j in range(4):
+        for i in range(j + 1):
             blk = jnp.concatenate([x_ref[k, :256, :], x_ref[k, 256:, :]], axis=1)
             if i == j:
                 blk = 0.5 * (blk + blk.T)
@@ -135,117 +135,228 @@
         out_specs=pl.BlockSpec((128, tk), lambda t: (0, t)),
         scratch_shapes=[pltpu.VMEM((256, 1024), BF)],
         compiler_params=pltpu.CompilerParams(vmem_limit_bytes=60<<20, dimension_semantics=("arbitrary",)))(f, u)
-F32 = jnp.float32
-STAGES = 5
+
 MESH = pl.DeviceIdType.MESH
+BLOCKS = [(i, j) for j in range(4) for i in range(j + 1)]
+STAGES = ((0, 3), (3, 6), (6, 8), (8, 9), (9, 10))
+KH = 2048
+TICKS = [(0, 0), (0, 1), (1, 0), (1, 1), (2, 0), (2, 1)] + [(k, h) for k in range(3, 10) for h in range(2)]
+
 
 class Net:
     def __init__(self):
         self.y = lax.axis_index("grp")
-        inn = lax.axis_index("in")
-        self.core = lax.rem(inn, 2)
-        self.x = lax.rem(inn // 2, 4)
-        self.z = inn // 8
-    def coord(self, axis):
-        return (self.x, self.y, self.z)[axis]
-    def step(self, axis, d):
-        return lax.rem(self.coord(axis) + d, 4)
-    def peer(self, axis, d):
-        c = [self.x, self.y, self.z]
-        c[axis] = self.step(axis, d)
-        return (c[1], (c[2] * 4 + c[0]) * 2 + self.core)
+        self.inn = lax.axis_index("in")
+        self.core = lax.rem(self.inn, 2)
+        self.x = lax.rem(self.inn // 2, 4)
+        self.z = self.inn // 8
+
+    def axis(self, number):
+        a = lax.rem(number, 3)
+        ex, ey, ez = (2 - a) * (1 - a) // 2, a * (2 - a), a * (a - 1) // 2
+        return Axis(self, ex, ey, ez)
+
     def twin(self):
-        return (self.y, (self.z * 4 + self.x) * 2 + 1 - self.core)
+        return (self.y, self.inn + 1 - 2 * self.core)
+
     def barrier(self):
         b = pltpu.get_barrier_semaphore()
         pl.semaphore_signal(b, inc=1, device_id=self.twin(), device_id_type=MESH)
-        for a in range(3):
+        for e in ((1, 0, 0), (0, 1, 0), (0, 0, 1)):
             for d in (1, 2, 3):
-                pl.semaphore_signal(b, inc=1, device_id=self.peer(a, d), device_id_type=MESH)
+                pl.semaphore_signal(b, inc=1, device_id=Axis(self, *e).peer(d), device_id_type=MESH)
         pl.semaphore_wait(b, 10)
 
-def ar_kernel(x_ref, o_ref, b0, b1, b2, b3, a0, a1, a2, ssem, rsem):
-    net = Net()
-    net.barrier()
-    def rc(src, dst, s, k, dev):
-        c = pltpu.make_async_remote_copy(src_ref=src, dst_ref=dst, send_sem=ssem.at[s, k], recv_sem=rsem.at[s, k], device_id=dev, device_id_type=MESH)
+
+class Axis:
+    def __init__(self, net, ex, ey, ez):
+        self.net, self.e = net, (ex, ey, ez)
+        self.me = net.x * ex + net.y * ey + net.z * ez
+
+    def at(self, d):
+        return lax.rem(self.me + d, 4)
+
+    def peer(self, d):
+        ex, ey, ez = self.e
+        delta = self.at(d) - self.me
+        return (self.net.y + delta * ey, self.net.inn + delta * (2 * ex + 8 * ez))
+
+
+def rows(start, n):
+    return pl.ds(pl.multiple_of(start, n), n)
+
+
+class Reduce:
+    def __init__(self, net, x, o, b0, a0, b1, a1, b2, a2, b3, ssem, rsem):
+        self.net, self.x, self.o = net, x, o
+        self.b0, self.a0, self.b1, self.a1, self.b2, self.a2, self.b3 = b0, a0, b1, a1, b2, a2, b3
+        self.ssem, self.rsem = ssem, rsem
+        self.flying, self.sent = {}, []
+        self.axes = {}
+        base = [net.axis(2 * net.core + e) for e in range(3)]
+        for s in range(len(STAGES)):
+            for p in range(2):
+                self.axes[s, p] = [base[(s + p + lvl) % 3] for lvl in range(3)]
+
+    def send(self, src, dst, s, k, dev):
+        c = pltpu.make_async_remote_copy(
+            src_ref=src, dst_ref=dst, send_sem=self.ssem.at[s, k], recv_sem=self.rsem.at[s, k],
+            device_id=dev, device_id_type=MESH,
+        )
         c.start()
-        return c
-    sent = []
-    order = [[(s + l) % 3 for l in range(3)] for s in range(STAGES)]
-    m = pl.multiple_of
-    cps = []
-    for s in range(STAGES):
-        cps.append([rc(x_ref.at[2 * s + 1 - net.core], b0.at[s], s, 0, net.twin())])
-    rows = (512, 128, 32, 8)
-    bufs = (b1, b2, b3)
-    accs = (a0, a1, a2)
-    for lvl in range(3):
-        n = rows[lvl + 1]
-        nxt = []
-        for s in range(STAGES):
-            for c in cps[s]:
-                c.wait_recv()
-            sent += cps[s]
-            acc = accs[lvl].at[s]
-            if lvl == 0:
-                acc[...] = x_ref[2 * s + net.core] + b0[s]
-            else:
-                p = net.coord(order[s][lvl - 1])
-                v = accs[lvl - 1][s, pl.ds(m(p * rows[lvl], rows[lvl]), rows[lvl]), :]
-                acc[...] = v + (bufs[lvl - 1][s, 0] + (bufs[lvl - 1][s, 1] + bufs[lvl - 1][s, 2]))
-            ax = order[s][lvl]
-            cur = []
-            for d in (1, 2, 3):
-                q = net.step(ax, d)
-                cur.append(rc(acc.at[pl.ds(m(q * n, n), n), :], bufs[lvl].at[s, d - 1], s, 3 * lvl + d, net.peer(ax, d)))
-            nxt.append(cur)
-        cps = nxt
-    offs = []
-    for s in range(STAGES):
-        c1, c2, c3 = (net.coord(a) for a in order[s])
-        offs.append((c1 * 128, c1 * 128 + c2 * 32, c1 * 128 + c2 * 32 + c3 * 8))
-    for lvl in (2, 1, 0):
-        n = rows[lvl + 1]
-        nxt = []
-        for s in range(STAGES):
-            for c in cps[s]:
-                c.wait_recv()
-            sent += cps[s]
-            unit = 2 * s + net.core
-            ax = order[s][lvl]
-            here = o_ref.at[unit, pl.ds(m(offs[s][lvl], n), n), :]
-            if lvl == 2:
-                p = net.coord(ax)
-                v = a2[s, pl.ds(m(p * 8, 8), 8), :]
-                here[...] = v + (b3[s, 0] + (b3[s, 1] + b3[s, 2]))
-            nxt.append([rc(here, here, s, 9 + 3 * lvl + d, net.peer(ax, d)) for d in (1, 2, 3)])
-        cps = nxt
-    nxt = []
-    for s in range(STAGES):
-        for c in cps[s]:
+        self.flying.setdefault(s, []).append(c)
+
+    def land(self, s):
+        for c in self.flying.get(s, []):
             c.wait_recv()
-        sent += cps[s]
-        unit = 2 * s + net.core
-        nxt.append(rc(o_ref.at[unit], o_ref.at[unit], s, 19, net.twin()))
-    for c in nxt:
-        c.wait_recv()
-    for c in sent + nxt:
-        c.wait_send()
-
-def allreduce(x):
+        self.sent += self.flying.get(s, [])
+        self.flying[s] = []
+
+    def step(self, s, phase):
+        u = slice(*STAGES[s])
+        core = self.net.core
+        self.land(s)
+        if phase == 0:
+            self.send(self.x.at[u, rows(256 - 256 * core, 256), :], self.b0.at[u], s, 0, self.net.twin())
+            return
+        if phase == 7:
+            half = self.o.at[u, rows(256 * core, 256), :]
+            self.send(half, half, s, 31, self.net.twin())
+            return
+        if phase == 8:
+            return
+        if phase == 1:
+            self.a0[u] = self.x[u, rows(256 * core, 256), :] + self.b0[u]
+        for p in range(2):
+            x1, x2, x3 = self.axes[s, p]
+            if phase == 1:
+                for d in (1, 2, 3):
+                    src = self.a0.at[u, rows(128 * p + 32 * x1.at(d), 32), :]
+                    self.send(src, self.b1.at[p, d - 1, u], s, 1 + 15 * p + d - 1, x1.peer(d))
+            if phase == 2:
+                own = self.a0[u, rows(128 * p + 32 * x1.me, 32), :]
+                self.a1[p, u] = own + (self.b1[p, 0, u] + (self.b1[p, 1, u] + self.b1[p, 2, u]))
+                for d in (1, 2, 3):
+                    src = self.a1.at[p, u, rows(8 * x2.at(d), 8), :]
+                    self.send(src, self.b2.at[p, d - 1, u], s, 4 + 15 * p + d - 1, x2.peer(d))
+            if phase == 3:
+                own = self.a1[p, u, rows(8 * x2.me, 8), :]
+                self.a2[p, u] = own + (self.b2[p, 0, u] + (self.b2[p, 1, u] + self.b2[p, 2, u]))
+                for d in (1, 2, 3):
+                    self.send(self.a2.at[p, u], self.b3.at[p, d - 1, u], s, 7 + 15 * p + d - 1, x3.peer(d))
+            if phase == 4:
+                here = self.o.at[u, rows(256 * core + 128 * p + 32 * x1.me + 8 * x2.me, 8), :]
+                here[...] = self.ordered(p, u, x3)
+                for d in (1, 2, 3):
+                    self.send(here, here, s, 10 + 15 * p + d - 1, x2.peer(d))
+            if phase == 5:
+                here = self.o.at[u, rows(256 * core + 128 * p + 32 * x1.me, 32), :]
+                for d in (1, 2, 3):
+                    self.send(here, here, s, 13 + 15 * p + d - 1, x1.peer(d))
+
+    def ordered(self, p, u, axis):
+        own, t1, t2, t3 = self.a2[p, u], self.b3[p, 0, u], self.b3[p, 1, u], self.b3[p, 2, u]
+        even = lax.rem(axis.me, 2) == 0
+        near = jnp.where(even, t3, t1)
+        far = jnp.where(even, t1, t3)
+        return (own + near) + (t2 + far)
+
+
+def plan(ticks):
+    ev = []
+    for s, (a, b) in enumerate(STAGES):
+        m = b - a
+        t = max(w for k, _, w in ticks if k < b)
+        cost = [1.0 + 0.3 * m, 2.2 + 0.85 * m, 2.2 + 0.2 * m, 2.2 + 0.2 * m, 2.2 + 0.2 * m, 2.2 + 0.85 * m, 0.0, 1.0 + 0.3 * m, 0.0]
+        for ph in (0, 1, 2, 3, 4, 5, 7, 8):
+            ev.append((t, s, ph))
+            t += cost[ph]
+    ev.sort()
+    return ev
+
+
+def gram_reduce_kernel(u_hbm, o_ref, stg, hl, x, b0, a0, b1, a1, b2, a2, b3, lsem, ssem, rsem, *, comm=True):
+    def load(n):
+        i, h = divmod(n, 2)
+        return pltpu.make_async_copy(
+            u_hbm.at[256 * i:256 * i + 256, KH * h:KH * h + KH], stg.at[n % 4], lsem.at[n % 4]
+        )
+    for n in range(4):
+        load(n).start()
+    if comm:
+        net = Net()
+        net.barrier()
+        red = Reduce(net, x, o_ref, b0, a0, b1, a1, b2, a2, b3, ssem, rsem)
+
+    def convert(n):
+        i, h = divmod(n, 2)
+        for c in range(0, KH, 256):
+            hi, lo = split(stg[n % 4, :, c:c + 256])
+            hl[i, :256, KH * h + c:KH * h + c + 256] = hi
+            hl[i, 256:, KH * h + c:KH * h + c + 256] = lo
+
+    ticks, t = [], 3.0
+    for n, (k, h) in enumerate(TICKS):
+        i, j = BLOCKS[k]
+        t += 0.275 * (2 if i == j else 3) + (0.8 if n < 7 else 0.0)
+        ticks.append((k, h, t))
+    events = plan(ticks) if comm else []
+    load(0).wait()
+    convert(0)
+    done = 1
+    for n, (k, h, t) in enumerate(ticks):
+        i, j = BLOCKS[k]
+        if done < 8:
+            if done >= 1 and done + 3 < 8:
+                load(done + 3).start()
+            load(done).wait()
+            convert(done)
+            done += 1
+        ks = slice(KH * h, KH * h + KH)
+        if i == j:
+            r = dg(hl[i, :256, ks], hl[j, :256, ks], 1, 1) + 2.0 * dg(hl[i, :256, ks], hl[j, 256:, ks], 1, 1)
+        else:
+            r2 = dg(hl[i, :, ks], hl[j, :256, ks], 1, 1)
+            r = r2[:256] + (r2[256:] + dg(hl[i, :256, ks], hl[j, 256:, ks], 1, 1))
+        dst = x if comm else o_ref
+        if h == 0:
+            dst[k, :256, :] = r[:, :128]
+            dst[k, 256:, :] = r[:, 128:]
+        else:
+            dst[k, :256, :] += r[:, :128]
+            dst[k, 256:, :] += r[:, 128:]
+        while events and events[0][0] <= t:
+            _, s, ph = events.pop(0)
+            red.step(s, ph)
+    for _, s, ph in events:
+        red.step(s, ph)
+    if comm:
+        for c in red.sent:
+            c.wait_send()
+
+
+def gram_reduce(u, comm=True):
     v = pl.BlockSpec(memory_space=pltpu.VMEM)
-    S = STAGES
-    return pl.pallas_call(ar_kernel, out_shape=jax.ShapeDtypeStruct((10, 512, 128), F32),
-        in_specs=[v], out_specs=v,
-        scratch_shapes=[pltpu.VMEM((S, 512, 128), F32), pltpu.VMEM((S, 3, 128, 128), F32), pltpu.VMEM((S, 3, 32, 128), F32), pltpu.VMEM((S, 3, 8, 128), F32),
-                        pltpu.VMEM((S, 512, 128), F32), pltpu.VMEM((S, 128, 128), F32), pltpu.VMEM((S, 32, 128), F32),
-                        pltpu.SemaphoreType.DMA((S, 20)), pltpu.SemaphoreType.DMA((S, 20))],
-        compiler_params=pltpu.CompilerParams(vmem_limit_bytes=60<<20, collective_id=0, has_side_effects=True))(x)
+    n = len(STAGES)
+    V = pltpu.VMEM
+    kw = dict(collective_id=0, has_side_effects=True) if comm else {}
+    return pl.pallas_call(
+        functools.partial(gram_reduce_kernel, comm=comm),
+        out_shape=jax.ShapeDtypeStruct((10, 512, 128), F32),
+        in_specs=[pl.BlockSpec(memory_space=pl.ANY)], out_specs=v,
+        scratch_shapes=[
+            V((4, 256, KH), F32), V((4, 512, 2 * KH), BF), V((10, 512, 128), F32),
+            V((10, 256, 128), F32), V((10, 256, 128), F32),
+            V((2, 3, 10, 32, 128), F32), V((2, 10, 32, 128), F32),
+            V((2, 3, 10, 8, 128), F32), V((2, 10, 8, 128), F32), V((2, 3, 10, 8, 128), F32),
+            pltpu.SemaphoreType.DMA((4,)), pltpu.SemaphoreType.DMA((n, 32)), pltpu.SemaphoreType.DMA((n, 32)),
+        ],
+        compiler_params=pltpu.CompilerParams(vmem_limit_bytes=60 << 20, **kw),
+    )(u)
 
 
 def per_device(unfolding, start_basis):
-    packed = allreduce(gram(unfolding))
+    packed = gram_reduce(unfolding)
     factor = k2(packed, start_basis)
     return factor, core(factor, unfolding, 1024)
 

time: 102 us -> 101 us (level)
  Pallas kernels: 102 us -> 100 us
    pallas_call x2 -> x1, Pallas kernels: 64.5 us -> 62.9 us  [gram_reduce(): pl.pallas_call(functools.partial(gram_reduce_kernel, comm=comm), out_shap...]
where the time goes in v2:
time: 101 us
  Pallas kernels  100 us (99%)
    pallas_call x1, Pallas kernels, gram_reduce(): pl.pallas_call(functools.partial(gram_reduce_kernel, comm=comm), out_shap...  62.9 us
    pallas_call x1, Pallas kernels, k2(): pl.pallas_call(functools.partial(k2_kernel, iters=iters), out_shape=jax.S...  27.6 us
    pallas_call x1, Pallas kernels, core(): pl.pallas_call(core_kernel, out_shape=jax.ShapeDtypeStruct((128, u.shape[...  9.46 us

profile of v2, /device:TPU:1, one launch (start us, length us, event | category | flops | bytes accessed | tf_op | source)
XLA Modules:
  0.0 100.7 jit_solution(13874340400444536202)
XLA Ops:
  0.6 62.9 %shard_map.41.x_ref = f32[10,512,128]{2,1,0:T(8,128)} custom-call(f32[1024,4096]{1,0:T(8,128)} %u_ref.1), custom_call_target="tpu_custom_call" | custom-call | tf_op jit(solution)/shard_map/pallas_call | solution.py:343
  63.6 27.6 %shard_map.42.f_ref = f32[1024,128]{1,0:T(8,128)} custom-call(f32[10,512,128]{2,1,0:T(8,128)} %shard_map.41.x_ref, f32[1024,128]{1,0:T(8,128)} %s_ref.1), custom_call_target="tpu_custom_call" | custom-call | tf_op jit(solution)/shard_map/pallas_call | solution.py:87
  91.2 9.5 %shard_map.43 = f32[128,4096]{1,0:T(8,128)} custom-call(f32[1024,128]{1,0:T(8,128)} %shard_map.42.f_ref, f32[1024,4096]{1,0:T(8,128)} %u_ref.1), custom_call_target="tpu_custom_call" | custom-call | tf_op jit(solution)/shard_map/pallas_call | solution.py:132

commit v3 on v2

--- a/solution.py
+++ b/solution.py
@@ -18,42 +18,110 @@
 def dg(a, b, ca, cb):
     return lax.dot_general(a, b, (((ca,), (cb,)), ((), ())), preferred_element_type=F32)
 
+GROUP = 8
+
+
 def eliminate(a_ref, q_ref, w_ref):
     sub = lax.broadcasted_iota(jnp.int32, (8, 128), 0)
     lane = lax.broadcasted_iota(jnp.int32, (8, 128), 1)
-    M = [a_ref[8*p:8*p+8, :] for p in range(16)]
-    Q = [jnp.where(lane == sub + 8*p, 1.0, 0.0).astype(F32) for p in range(16)]
+    wide = lambda v: jnp.broadcast_to(v, (8, 128))
+    row = lambda v, r: wide(v[r:r + 1, :])
+    col = lambda v, c: wide(v[:, c:c + 1])
+    M = [a_ref[8 * p:8 * p + 8, :] for p in range(16)]
+    on = [lane == sub + 8 * p for p in range(16)]
+    diag = jnp.where(on[0], M[0], 0.0)
+    for p in range(1, 16):
+        diag = diag + jnp.where(on[p], M[p], 0.0)
+    scale = wide(1.0 / jnp.sqrt(jnp.sum(diag, axis=0, keepdims=True)))
+    Q = [jnp.where(on[p], scale, 0.0) for p in range(16)]
+    for p in range(16):
+        M[p] = M[p] * scale * wide(jnp.sum(Q[p], axis=1, keepdims=True))
+    done = []
     for p in range(16):
         P, R = M[p], Q[p]
-        cols = [jnp.broadcast_to(P[:, 8*p+c:8*p+c+1], (8, 128)) for c in range(8)]
-        piv = []
-        recs = []
-        for r in range(8):
-            d = jnp.broadcast_to(cols[r][r:r+1, :], (8, 128))
-            rec = 1.0 / d
-            piv.append(d); recs.append(rec)
-            if r == 7: break
-            m = jnp.where(sub > r, cols[r] * rec, 0.0)
-            for c in range(r+1, 8):
-                cols[c] = cols[c] - m * jnp.broadcast_to(cols[c][r:r+1, :], (8, 128))
-            P = P - m * jnp.broadcast_to(P[r:r+1, :], (8, 128))
-            R = R - m * jnp.broadcast_to(R[r:r+1, :], (8, 128))
-        dv = piv[7]; rv = recs[7]
-        for r in range(7):
-            dv = jnp.where(sub == r, piv[r], dv)
-            rv = jnp.where(sub == r, recs[r], rv)
-        w_ref[8*p:8*p+8, :] = R * (1.0 / jnp.sqrt(dv))
-        if p < 15:
+        last = p == 15
+        edge = p % GROUP == GROUP - 1
+        N, S = (None, None) if edge else (M[p + 1], Q[p + 1])
+        cs = [col(P, 8 * p + c) for c in range(8)] if p % GROUP == 0 else gs
+        es, fs, gs = [], [], []
+        if not edge:
+            es = [col(N, 8 * p + c) for c in range(8)]
+            fs = [col(P, 8 * p + 8 + c) for c in range(8)]
+            gs = [col(N, 8 * p + 8 + c) for c in range(8)]
+        dv = rv = tv = jnp.zeros((8, 128), F32)
+        for r in range(0, 8, 2):
+            a, b, d = row(cs[r], r), row(cs[r], r + 1), row(cs[r + 1], r + 1)
+            det = a * d - b * b
+            rdet = 1.0 / det
+            ra = 1.0 / a
+            dv = jnp.where(sub == r, a, jnp.where(sub == r + 1, det * ra, dv))
+            rv = jnp.where(sub == r, ra, jnp.where(sub == r + 1, a * rdet, rv))
+            tv = jnp.where(sub == r + 1, b * ra, tv)
+            sets = []
+            if r < 6:
+                below = sub > r + 1
+                sets.append((jnp.where(below, d * cs[r] - b * cs[r + 1], 0.0),
+                             jnp.where(below, a * cs[r + 1] - b * cs[r], 0.0)))
+            if not edge:
+                sets.append((d * es[r] - b * es[r + 1], a * es[r + 1] - b * es[r]))
+            p0, p1, q0, q1 = row(P, r), row(P, r + 1), row(R, r), row(R, r + 1)
+            for k in range(r + 2, 8):
+                s0, s1 = row(cs[k], r), row(cs[k], r + 1)
+                if not edge:
+                    n0, n1 = sets[-1]
+                    es[k] = es[k] - rdet * (n0 * s0 + n1 * s1)
+                n0, n1 = sets[0]
+                cs[k] = cs[k] - rdet * (n0 * s0 + n1 * s1)
+            for k in range(8 if not edge else 0):
+                s0, s1 = row(fs[k], r), row(fs[k], r + 1)
+                n0, n1 = sets[-1]
+                gs[k] = gs[k] - rdet * (n0 * s0 + n1 * s1)
+                if r < 6:
+                    n0, n1 = sets[0]
+                    fs[k] = fs[k] - rdet * (n0 * s0 + n1 * s1)
+            if r < 6:
+                n0, n1 = sets[0]
+                P = P - rdet * (n0 * p0 + n1 * p1)
+                R = R - rdet * (n0 * q0 + n1 * q1)
+            if not edge:
+                n0, n1 = sets[-1]
+                N = N - rdet * (n0 * p0 + n1 * p1)
+                S = S - rdet * (n0 * q0 + n1 * q1)
+        P = P - tv * pltpu.roll(P, 1, 0)
+        R = R - tv * pltpu.roll(R, 1, 0)
+        w_ref[8 * p:8 * p + 8, :] = R * (1.0 / jnp.sqrt(dv))
+        if not edge:
+            M[p + 1], Q[p + 1] = N, S
+        done.append((P, R, P * rv))
+        group = p // GROUP
+        stop = GROUP * group + GROUP
+        if p + 2 < min(stop, 16):
             T = jnp.transpose(P * rv)
-            pr = [jnp.broadcast_to(P[r:r+1, :], (8, 128)) for r in range(8)]
-            qr = [jnp.broadcast_to(R[r:r+1, :], (8, 128)) for r in range(8)]
-            for i in range(p+1, 16):
+            pr = [row(P, r) for r in range(8)]
+            qr = [row(R, r) for r in range(8)]
+            for i in range(p + 2, stop):
                 for r in range(8):
-                    mm = jnp.broadcast_to(T[8*i:8*i+8, r:r+1], (8, 128))
+                    mm = wide(T[8 * i:8 * i + 8, r:r + 1])
                     M[i] = M[i] - mm * pr[r]
                     Q[i] = Q[i] - mm * qr[r]
-
-def k2_kernel(x_ref, s_ref, f_ref, ghi, glo, img, a_ref, q_ref, w_ref, *, iters=3):
+        if p == stop - 1 and not last:
+            parts = done[GROUP * group:]
+            left = jnp.concatenate([v[2] for v in parts], axis=0)
+            right = jnp.concatenate([jnp.concatenate(v[:2], axis=1) for v in parts], axis=0)
+            upd = lax.dot_general(left, right, (((0,), (0,)), ((), ())), precision=HI, preferred_element_type=F32)
+            for i in range(stop, 16):
+                M[i] = M[i] - upd[8 * i:8 * i + 8, :128]
+                Q[i] = Q[i] - upd[8 * i:8 * i + 8, 128:]
+
+
+ITERS = 3
+
+
+def tail_kernel(x_ref, s_ref, u_hbm, f_ref, o_hbm, ghi, glo, img, a_ref, q_ref, w_ref, u_ref, f2, out, lsem, osem):
+    pieces = [slice(c, c + 512) for c in range(0, 4096, 512)]
+    loads = [pltpu.make_async_copy(u_hbm.at[:, c], u_ref.at[:, c], lsem.at[n]) for n, c in enumerate(pieces)]
+    for c in loads:
+        c.start()
     k = 0
     for j in range(4):
         for i in range(j + 1):
@@ -68,6 +136,7 @@
                 glo[256*j:256*j+256, 256*i:256*i+256] = lo.T
             k += 1
     f_ref[...] = s_ref[...]
+
     def body(t, _):
         bh, bl = split(f_ref[...])
         b2 = jnp.concatenate([bh, bl], axis=1)
@@ -80,66 +149,45 @@
         eliminate(a_ref, q_ref, w_ref)
         f_ref[...] = lax.dot_general(img[...], w_ref[...], (((1,), (1,)), ((), ())), precision=HI, preferred_element_type=F32)
         return 0
-    lax.fori_loop(0, iters, body, 0)
-
-def k2(x, s, iters=3):
-    v = pl.BlockSpec(memory_space=pltpu.VMEM)
-    return pl.pallas_call(functools.partial(k2_kernel, iters=iters), out_shape=jax.ShapeDtypeStruct((1024, 128), F32),
-        in_specs=[v, v], out_specs=v,
-        scratch_shapes=[pltpu.VMEM((1024,1024),BF), pltpu.VMEM((1024,1024),BF), pltpu.VMEM((1024,128),F32),
-                        pltpu.VMEM((128,128),F32), pltpu.VMEM((128,128),F32), pltpu.VMEM((128,128),F32)],
-        compiler_params=pltpu.CompilerParams(vmem_limit_bytes=60<<20))(x, s)
-
-def gram_kernel(u_ref, o_ref, h_ref, l_ref):
-    t = pl.program_id(0)
-    h, l = split(u_ref[...])
-    h_ref[...] = h; l_ref[...] = l
-    @pl.when(t == 0)
-    def _(): o_ref[...] = jnp.zeros_like(o_ref)
-    k = 0
-    for i in range(4):
-        for j in range(i, 4):
-            hi, hj = h_ref[256*i:256*i+256, :], h_ref[256*j:256*j+256, :]
-            li, lj = l_ref[256*i:256*i+256, :], l_ref[256*j:256*j+256, :]
-            r = dg(hi, hj, 1, 1)
-            if i == j:
-                r = r + 2.0 * dg(hi, lj, 1, 1)
-            else:
-                r = r + (dg(hi, lj, 1, 1) + dg(li, hj, 1, 1))
-            o_ref[k, :256, :] += r[:, :128]
-            o_ref[k, 256:, :] += r[:, 128:]
-            k += 1
-
-def gram(u, tk=512):
-    return pl.pallas_call(gram_kernel, out_shape=jax.ShapeDtypeStruct((10, 512, 128), F32),
-        grid=(u.shape[1]//tk,),
-        in_specs=[pl.BlockSpec((1024, tk), lambda t: (0, t))],
-        out_specs=pl.BlockSpec((10, 512, 128), lambda t: (0, 0, 0)),
-        scratch_shapes=[pltpu.VMEM((1024, tk), BF), pltpu.VMEM((1024, tk), BF)],
-        compiler_params=pltpu.CompilerParams(vmem_limit_bytes=60<<20, dimension_semantics=("arbitrary",)))(u)
-
-def core_kernel(f_ref, u_ref, o_ref, f2_ref):
-    @pl.when(pl.program_id(0) == 0)
-    def _():
-        ft = f_ref[...].T
-        fh, fl = split(ft)
-        f2_ref[:128, :] = fh; f2_ref[128:, :] = fl
-    h, l = split(u_ref[...])
-    r = dg(f2_ref[...], h, 1, 0)
-    o_ref[...] = r[:128, :] + (r[128:, :] + dg(f2_ref[:128, :], l, 1, 0))
-
-def core(f, u, tk=512):
-    return pl.pallas_call(core_kernel, out_shape=jax.ShapeDtypeStruct((128, u.shape[1]), F32),
-        grid=(u.shape[1]//tk,),
-        in_specs=[pl.BlockSpec((1024, 128), lambda t: (0, 0)), pl.BlockSpec((1024, tk), lambda t: (0, t))],
-        out_specs=pl.BlockSpec((128, tk), lambda t: (0, t)),
-        scratch_shapes=[pltpu.VMEM((256, 1024), BF)],
-        compiler_params=pltpu.CompilerParams(vmem_limit_bytes=60<<20, dimension_semantics=("arbitrary",)))(f, u)
+
+    lax.fori_loop(0, ITERS, body, 0)
+    fh, fl = split(f_ref[...].T)
+    f2[:128, :] = fh
+    f2[128:, :] = fl
+    for c in loads:
+        c.wait()
+    stores = []
+    for n, c in enumerate(pieces):
+        h, l = split(u_ref[:, c])
+        r = dg(f2[...], h, 1, 0)
+        out[:, c] = r[:128, :] + (r[128:, :] + dg(f2[:128, :], l, 1, 0))
+        if n % 2 == 1:
+            two = slice(c.stop - 1024, c.stop)
+            stores.append(pltpu.make_async_copy(out.at[:, two], o_hbm.at[:, two], osem.at[n // 2]))
+            stores[-1].start()
+    for c in stores:
+        c.wait()
+
+
+def iterate_project(x, s, u):
+    v, anyw = pl.BlockSpec(memory_space=pltpu.VMEM), pl.BlockSpec(memory_space=pl.ANY)
+    V = pltpu.VMEM
+    return pl.pallas_call(
+        tail_kernel,
+        out_shape=(jax.ShapeDtypeStruct((1024, 128), F32), jax.ShapeDtypeStruct((128, 4096), F32)),
+        in_specs=[v, v, anyw], out_specs=(v, anyw),
+        scratch_shapes=[V((1024, 1024), BF), V((1024, 1024), BF), V((1024, 128), F32),
+                        V((128, 128), F32), V((128, 128), F32), V((128, 128), F32),
+                        V((1024, 4096), F32), V((256, 1024), BF), V((128, 4096), F32),
+                        pltpu.SemaphoreType.DMA((8,)), pltpu.SemaphoreType.DMA((4,))],
+        compiler_params=pltpu.CompilerParams(vmem_limit_bytes=60 << 20),
+    )(x, s, u)
 
 MESH = pl.DeviceIdType.MESH
 BLOCKS = [(i, j) for j in range(4) for i in range(j + 1)]
 STAGES = ((0, 3), (3, 6), (6, 8), (8, 9), (9, 10))
 KH = 2048
+LAT = (2.0, 3.9, 3.0)
 TICKS = [(0, 0), (0, 1), (1, 0), (1, 1), (2, 0), (2, 1)] + [(k, h) for k in range(3, 10) for h in range(2)]
 
 
@@ -267,7 +315,7 @@
     for s, (a, b) in enumerate(STAGES):
         m = b - a
         t = max(w for k, _, w in ticks if k < b)
-        cost = [1.0 + 0.3 * m, 2.2 + 0.85 * m, 2.2 + 0.2 * m, 2.2 + 0.2 * m, 2.2 + 0.2 * m, 2.2 + 0.85 * m, 0.0, 1.0 + 0.3 * m, 0.0]
+        cost = [LAT[0] + 0.3 * m, LAT[1] + 0.85 * m, LAT[1] + 0.25 * m, LAT[2] + 0.25 * m, LAT[1] + 0.25 * m, LAT[1] + 0.85 * m, 0.0, LAT[0] + 0.3 * m, 0.0]
         for ph in (0, 1, 2, 3, 4, 5, 7, 8):
             ev.append((t, s, ph))
             t += cost[ph]
@@ -357,8 +405,7 @@
 
 def per_device(unfolding, start_basis):
     packed = gram_reduce(unfolding)
-    factor = k2(packed, start_basis)
-    return factor, core(factor, unfolding, 1024)
+    return iterate_project(packed, start_basis, unfolding)
 
 
 def solution(mesh):

time: 101 us -> 88.4 us (0.88)
  Pallas kernels: 100 us -> 87.5 us
    pallas_call x2 -> x1, Pallas kernels: 37.1 us -> 27.6 us  [iterate_project(): pl.pallas_call(tail_kernel, out_shape=(jax.ShapeDtypeStruct((1024, 128),...]
    pallas_call x1, Pallas kernels: 62.9 us -> 59.9 us  [gram_reduce(): pl.pallas_call(functools.partial(gram_reduce_kernel, comm=comm), out_shap...]
where the time goes in v3:
time: 88.4 us; the launch traced here: 88.3 us
  Pallas kernels  87.5 us (99%)
    pallas_call x1, Pallas kernels, gram_reduce(): pl.pallas_call(functools.partial(gram_reduce_kernel, comm=comm), out_shap...  59.9 us
    pallas_call x1, Pallas kernels, iterate_project(): pl.pallas_call(tail_kernel, out_shape=(jax.ShapeDtypeStruct((1024, 128),...  27.6 us

profile of v3, /device:TPU:1, one launch (start us, length us, event | category | flops | bytes accessed | tf_op | source)
XLA Modules:
  0.0 88.3 jit_solution(5342531568641604881)
XLA Ops:
  0.6 59.9 %shard_map.41.x_ref = f32[10,512,128]{2,1,0:T(8,128)} custom-call(f32[1024,4096]{1,0:T(8,128)} %u_hbm.3), custom_call_target="tpu_custom_call" | custom-call | tf_op jit(solution)/shard_map/pallas_call | solution.py:391
  60.6 27.6 %shard_map.42 = (f32[1024,128]{1,0:T(8,128)}, f32[128,4096]{1,0:T(8,128)}) custom-call(f32[10,512,128]{2,1,0:T(8,128)} %shard_map.41.x_ref, f32[1024,128]{1,0:T(8,128)} %s_ref.1, f32[1024,4096]{1,0:T(8,128)} %u_hbm.3), custom_call_target="tpu_custom_call" | custom-call | tf_op jit(solution)/shard_map/pallas_call | solution.py:175

commit v4 on v3

--- a/solution.py
+++ b/solution.py
@@ -180,15 +180,15 @@
                         V((128, 128), F32), V((128, 128), F32), V((128, 128), F32),
                         V((1024, 4096), F32), V((256, 1024), BF), V((128, 4096), F32),
                         pltpu.SemaphoreType.DMA((8,)), pltpu.SemaphoreType.DMA((4,))],
-        compiler_params=pltpu.CompilerParams(vmem_limit_bytes=60 << 20),
+        compiler_params=pltpu.CompilerParams(vmem_limit_bytes=50 << 20),
     )(x, s, u)
 
 MESH = pl.DeviceIdType.MESH
 BLOCKS = [(i, j) for j in range(4) for i in range(j + 1)]
-STAGES = ((0, 3), (3, 6), (6, 8), (8, 9), (9, 10))
+STAGES = ((0, 3), (3, 6), (6, 8), (8, 10))
 KH = 2048
+ORDER = True
 LAT = (2.0, 3.9, 3.0)
-TICKS = [(0, 0), (0, 1), (1, 0), (1, 1), (2, 0), (2, 1)] + [(k, h) for k in range(3, 10) for h in range(2)]
 
 
 class Net:
@@ -310,74 +310,90 @@
         return (own + near) + (t2 + far)
 
 
-def plan(ticks):
-    ev = []
+PROGRAM = (
+    ("wait", 0), ("convert", 0, 0),
+    ("wait", 1), ("convert", 0, 1), ("dot", 0, 0), ("dot", 0, 1),
+    ("wait", 2), ("convert", 1, 0), ("dot", 1, 0), ("dot", 2, 0), ("convert", 1, 1),
+    ("wait", 3), ("dot", 1, 1), ("dot", 2, 1), ("convert", 2, 0), ("check", 3, 7.5),
+    ("wait", 4), ("convert", 2, 1), ("dot", 3, 2), ("dot", 4, 2), ("convert", 3, 0), ("check", 5, 11.0),
+    ("dot", 5, 2), ("convert", 3, 1), ("check", 6, 12.4),
+    ("dot", 6, 2), ("dot", 7, 2), ("check", 8, 15.7),
+    ("dot", 8, 2), ("check", 9, 17.4),
+    ("dot", 9, 2), ("check", 10, 18.5),
+)
+
+
+def plan():
+    ready = {}
+    for op in PROGRAM:
+        if op[0] == "check":
+            for k in range(op[1]):
+                ready.setdefault(k, op[2])
+    steps = []
     for s, (a, b) in enumerate(STAGES):
         m = b - a
-        t = max(w for k, _, w in ticks if k < b)
-        cost = [LAT[0] + 0.3 * m, LAT[1] + 0.85 * m, LAT[1] + 0.25 * m, LAT[2] + 0.25 * m, LAT[1] + 0.25 * m, LAT[1] + 0.85 * m, 0.0, LAT[0] + 0.3 * m, 0.0]
+        t = ready[b - 1]
+        cost = (LAT[0] + 0.3 * m, LAT[1] + 0.6 * m, LAT[1] + 0.2 * m, LAT[2] + 0.2 * m, LAT[1] + 0.2 * m, LAT[1] + 0.6 * m, 0.0, LAT[0] + 0.3 * m, 0.0)
         for ph in (0, 1, 2, 3, 4, 5, 7, 8):
-            ev.append((t, s, ph))
+            steps.append((t, s, ph))
             t += cost[ph]
-    ev.sort()
-    return ev
+    return sorted(steps)
 
 
 def gram_reduce_kernel(u_hbm, o_ref, stg, hl, x, b0, a0, b1, a1, b2, a2, b3, lsem, ssem, rsem, *, comm=True):
-    def load(n):
-        i, h = divmod(n, 2)
-        return pltpu.make_async_copy(
-            u_hbm.at[256 * i:256 * i + 256, KH * h:KH * h + KH], stg.at[n % 4], lsem.at[n % 4]
-        )
-    for n in range(4):
-        load(n).start()
+    cuts = [(0, 256, 0, 2048), (0, 256, 2048, 4096), (256, 512, 0, 4096), (512, 768, 0, 4096), (768, 1024, 0, 4096)]
+    loads = []
+    for n, (ra, rb, ca, cb) in enumerate(cuts):
+        loads.append(pltpu.make_async_copy(u_hbm.at[ra:rb, ca:cb], stg.at[ra:rb, ca:cb], lsem.at[n]))
+        loads[-1].start()
+    steps = []
     if comm:
         net = Net()
         net.barrier()
         red = Reduce(net, x, o_ref, b0, a0, b1, a1, b2, a2, b3, ssem, rsem)
-
-    def convert(n):
-        i, h = divmod(n, 2)
-        for c in range(0, KH, 256):
-            hi, lo = split(stg[n % 4, :, c:c + 256])
-            hl[i, :256, KH * h + c:KH * h + c + 256] = hi
-            hl[i, 256:, KH * h + c:KH * h + c + 256] = lo
-
-    ticks, t = [], 3.0
-    for n, (k, h) in enumerate(TICKS):
+        steps = plan()
+
+    def convert(i, h):
+        for c in range(KH * h, KH * h + KH, 256):
+            hi, lo = split(stg[256 * i:256 * i + 256, c:c + 256])
+            hl[i, :256, c:c + 256] = hi
+            hl[i, 256:, c:c + 256] = lo
+
+    dst = x if comm else o_ref
+
+    def dot(k, h):
         i, j = BLOCKS[k]
-        t += 0.275 * (2 if i == j else 3) + (0.8 if n < 7 else 0.0)
-        ticks.append((k, h, t))
-    events = plan(ticks) if comm else []
-    load(0).wait()
-    convert(0)
-    done = 1
-    for n, (k, h, t) in enumerate(ticks):
-        i, j = BLOCKS[k]
-        if done < 8:
-            if done >= 1 and done + 3 < 8:
-                load(done + 3).start()
-            load(done).wait()
-            convert(done)
-            done += 1
-        ks = slice(KH * h, KH * h + KH)
+        ks = slice(0, 2 * KH) if h == 2 else slice(KH * h, KH * h + KH)
         if i == j:
             r = dg(hl[i, :256, ks], hl[j, :256, ks], 1, 1) + 2.0 * dg(hl[i, :256, ks], hl[j, 256:, ks], 1, 1)
         else:
             r2 = dg(hl[i, :, ks], hl[j, :256, ks], 1, 1)
             r = r2[:256] + (r2[256:] + dg(hl[i, :256, ks], hl[j, 256:, ks], 1, 1))
-        dst = x if comm else o_ref
-        if h == 0:
+        if h == 1:
+            dst[k, :256, :] += r[:, :128]
+            dst[k, 256:, :] += r[:, 128:]
+        else:
             dst[k, :256, :] = r[:, :128]
             dst[k, 256:, :] = r[:, 128:]
+
+    for op in PROGRAM:
+        if op[0] == "wait":
+            loads[op[1]].wait()
+        elif op[0] == "convert":
+            convert(*op[1:])
+        elif op[0] == "dot":
+            dot(*op[1:])
         else:
-            dst[k, :256, :] += r[:, :128]
-            dst[k, 256:, :] += r[:, 128:]
-        while events and events[0][0] <= t:
-            _, s, ph = events.pop(0)
-            red.step(s, ph)
-    for _, s, ph in events:
-        red.step(s, ph)
+            while steps and steps[0][0] <= op[2] + 0.01:
+                _, s, ph = steps.pop(0)
+                red.step(s, ph)
+    left = {}
+    for _, s, ph in steps:
+        left.setdefault(s, []).append(ph)
+    while any(left.values()):
+        for s in sorted(left, reverse=ORDER):
+            if left[s]:
+                red.step(s, left[s].pop(0))
     if comm:
         for c in red.sent:
             c.wait_send()
@@ -393,13 +409,13 @@
         out_shape=jax.ShapeDtypeStruct((10, 512, 128), F32),
         in_specs=[pl.BlockSpec(memory_space=pl.ANY)], out_specs=v,
         scratch_shapes=[
-            V((4, 256, KH), F32), V((4, 512, 2 * KH), BF), V((10, 512, 128), F32),
+            V((1024, 2 * KH), F32), V((4, 512, 2 * KH), BF), V((10, 512, 128), F32),
             V((10, 256, 128), F32), V((10, 256, 128), F32),
             V((2, 3, 10, 32, 128), F32), V((2, 10, 32, 128), F32),
             V((2, 3, 10, 8, 128), F32), V((2, 10, 8, 128), F32), V((2, 3, 10, 8, 128), F32),
-            pltpu.SemaphoreType.DMA((4,)), pltpu.SemaphoreType.DMA((n, 32)), pltpu.SemaphoreType.DMA((n, 32)),
+            pltpu.SemaphoreType.DMA((5,)), pltpu.SemaphoreType.DMA((n, 32)), pltpu.SemaphoreType.DMA((n, 32)),
         ],
-        compiler_params=pltpu.CompilerParams(vmem_limit_bytes=60 << 20, **kw),
+        compiler_params=pltpu.CompilerParams(vmem_limit_bytes=46 << 20, **kw),
     )(u)
 
 

time: 88.4 us -> 81.5 us (0.922)
  Pallas kernels: 87.5 us -> 80.6 us
    pallas_call x1, Pallas kernels: 59.9 us -> 54.9 us  [gram_reduce(): pl.pallas_call(functools.partial(gram_reduce_kernel, comm=comm), out_shap...]
    pallas_call x1, Pallas kernels: 27.6 us -> 25.7 us  [iterate_project(): pl.pallas_call(tail_kernel, out_shape=(jax.ShapeDtypeStruct((1024, 128),...]
where the time goes in v4:
time: 81.5 us; the launch traced here: 81.4 us
  Pallas kernels  80.6 us (99%)
    pallas_call x1, Pallas kernels, gram_reduce(): pl.pallas_call(functools.partial(gram_reduce_kernel, comm=comm), out_shap...  54.9 us
    pallas_call x1, Pallas kernels, iterate_project(): pl.pallas_call(tail_kernel, out_shape=(jax.ShapeDtypeStruct((1024, 128),...  25.7 us

profile of v4, /device:TPU:1, one launch (start us, length us, event | category | flops | bytes accessed | tf_op | source)
XLA Modules:
  0.0 81.4 jit_solution(255838701063539169)
XLA Ops:
  0.6 0.0 copy-start
  0.6 54.9 %shard_map.41.x_ref = f32[10,512,128]{2,1,0:T(8,128)S(1)} custom-call(f32[1024,4096]{1,0:T(8,128)} %u_hbm.3), custom_call_target="tpu_custom_call" | custom-call | tf_op jit(solution)/shard_map/pallas_call | solution.py:407
  55.5 0.0 copy-done
  55.5 25.7 %shard_map.42 = (f32[1024,128]{1,0:T(8,128)}, f32[128,4096]{1,0:T(8,128)}) custom-call(f32[10,512,128]{2,1,0:T(8,128)S(1)} %shard_map.41.x_ref, f32[1024,128]{1,0:T(8,128)S(1)} %copy-done, f32[1024,4096]{1,0:T(8,128)} %u_hbm.3), custom_call_target="tpu_custom_call" | custom-call | tf_op jit(solution)/shard_map/pallas_call | solution.py:175
Async XLA Ops:
  0.6 54.9 %copy-start = (f32[1024,128]{1,0:T(8,128)S(1)}, f32[1024,128]{1,0:T(8,128)}, u32[]{:S(2)}) copy-start(f32[1024,128]{1,0:T(8,128)} %s_ref.1) | copy-start | bytes 1572868

commit v5 on v4

--- a/solution.py
+++ b/solution.py
@@ -43,10 +43,9 @@
         edge = p % GROUP == GROUP - 1
         N, S = (None, None) if edge else (M[p + 1], Q[p + 1])
         cs = [col(P, 8 * p + c) for c in range(8)] if p % GROUP == 0 else gs
-        es, fs, gs = [], [], []
+        es, gs = [], []
         if not edge:
             es = [col(N, 8 * p + c) for c in range(8)]
-            fs = [col(P, 8 * p + 8 + c) for c in range(8)]
             gs = [col(N, 8 * p + 8 + c) for c in range(8)]
         dv = rv = tv = jnp.zeros((8, 128), F32)
         for r in range(0, 8, 2):
@@ -73,12 +72,9 @@
                 n0, n1 = sets[0]
                 cs[k] = cs[k] - rdet * (n0 * s0 + n1 * s1)
             for k in range(8 if not edge else 0):
-                s0, s1 = row(fs[k], r), row(fs[k], r + 1)
+                s0, s1 = row(es[r], k), row(es[r + 1], k)
                 n0, n1 = sets[-1]
                 gs[k] = gs[k] - rdet * (n0 * s0 + n1 * s1)
-                if r < 6:
-                    n0, n1 = sets[0]
-                    fs[k] = fs[k] - rdet * (n0 * s0 + n1 * s1)
             if r < 6:
                 n0, n1 = sets[0]
                 P = P - rdet * (n0 * p0 + n1 * p1)
@@ -207,13 +203,15 @@
     def twin(self):
         return (self.y, self.inn + 1 - 2 * self.core)
 
-    def barrier(self):
+    def greet(self):
         b = pltpu.get_barrier_semaphore()
         pl.semaphore_signal(b, inc=1, device_id=self.twin(), device_id_type=MESH)
         for e in ((1, 0, 0), (0, 1, 0), (0, 0, 1)):
             for d in (1, 2, 3):
                 pl.semaphore_signal(b, inc=1, device_id=Axis(self, *e).peer(d), device_id_type=MESH)
-        pl.semaphore_wait(b, 10)
+
+    def meet(self):
+        pl.semaphore_wait(pltpu.get_barrier_semaphore(), 10)
 
 
 class Axis:
@@ -349,7 +347,7 @@
     steps = []
     if comm:
         net = Net()
-        net.barrier()
+        net.greet()
         red = Reduce(net, x, o_ref, b0, a0, b1, a1, b2, a2, b3, ssem, rsem)
         steps = plan()
 
@@ -384,6 +382,8 @@
         elif op[0] == "dot":
             dot(*op[1:])
         else:
+            if comm and op[1] == 3:
+                net.meet()
             while steps and steps[0][0] <= op[2] + 0.01:
                 _, s, ph = steps.pop(0)
                 red.step(s, ph)

time: 81.5 us -> 80.7 us (level)
    pallas_call x1, Pallas kernels: 25.7 us -> 24.9 us  [iterate_project(): pl.pallas_call(tail_kernel, out_shape=(jax.ShapeDtypeStruct((1024, 128),...]
where the time goes in v5:
time: 80.7 us; the launch traced here: 80.6 us
  Pallas kernels  79.8 us (99%)
  between operations  0.81 us (1%)
    pallas_call x1, Pallas kernels, gram_reduce(): pl.pallas_call(functools.partial(gram_reduce_kernel, comm=comm), out_shap...  54.9 us
    pallas_call x1, Pallas kernels, iterate_project(): pl.pallas_call(tail_kernel, out_shape=(jax.ShapeDtypeStruct((1024, 128),...  24.9 us

profile of v5, /device:TPU:1, one launch (start us, length us, event | category | flops | bytes accessed | tf_op | source)
XLA Modules:
  0.0 80.6 jit_solution(16153671647351492845)
XLA Ops:
  0.6 0.0 copy-start
  0.6 54.9 %shard_map.41.x_ref = f32[10,512,128]{2,1,0:T(8,128)S(1)} custom-call(f32[1024,4096]{1,0:T(8,128)} %u_hbm.3), custom_call_target="tpu_custom_call" | custom-call | tf_op jit(solution)/shard_map/pallas_call | solution.py:407
  55.6 0.0 copy-done
  55.6 24.9 %shard_map.42 = (f32[1024,128]{1,0:T(8,128)}, f32[128,4096]{1,0:T(8,128)}) custom-call(f32[10,512,128]{2,1,0:T(8,128)S(1)} %shard_map.41.x_ref, f32[1024,128]{1,0:T(8,128)S(1)} %copy-done, f32[1024,4096]{1,0:T(8,128)} %u_hbm.3), custom_call_target="tpu_custom_call" | custom-call | tf_op jit(solution)/shard_map/pallas_call | solution.py:171
Async XLA Ops:
  0.6 54.9 %copy-start = (f32[1024,128]{1,0:T(8,128)S(1)}, f32[1024,128]{1,0:T(8,128)}, u32[]{:S(2)}) copy-start(f32[1024,128]{1,0:T(8,128)} %s_ref.1) | copy-start | bytes 1572868

commit v6 on v5

--- a/solution.py
+++ b/solution.py
@@ -143,7 +143,10 @@
         im = img[...]
         a_ref[...] = lax.dot_general(im, im, (((0,), (0,)), ((), ())), precision=HI, preferred_element_type=F32)
         eliminate(a_ref, q_ref, w_ref)
-        f_ref[...] = lax.dot_general(img[...], w_ref[...], (((1,), (1,)), ((), ())), precision=HI, preferred_element_type=F32)
+        ih, il = split(img[...])
+        wh, wl = split(w_ref[...])
+        r2 = dg(ih, jnp.concatenate([wh, wl], axis=0), 1, 1)
+        f_ref[...] = r2[:, :128] + (r2[:, 128:] + dg(il, wh, 1, 1))
         return 0
 
     lax.fori_loop(0, ITERS, body, 0)

time: 80.7 us -> 79.9 us (0.990)
    pallas_call x1, Pallas kernels: 24.9 us -> 24.1 us  [iterate_project(): pl.pallas_call(tail_kernel, out_shape=(jax.ShapeDtypeStruct((1024, 128),...]
where the time goes in v6:
time: 79.9 us; the launch traced here: 79.8 us
  Pallas kernels  79 us (99%)
  between operations  0.81 us (1%)
    pallas_call x1, Pallas kernels, gram_reduce(): pl.pallas_call(functools.partial(gram_reduce_kernel, comm=comm), out_shap...  54.9 us
    pallas_call x1, Pallas kernels, iterate_project(): pl.pallas_call(tail_kernel, out_shape=(jax.ShapeDtypeStruct((1024, 128),...  24.1 us

profile of v6, /device:TPU:1, one launch (start us, length us, event | category | flops | bytes accessed | tf_op | source)
XLA Modules:
  0.0 79.8 jit_solution(7707321566462690730)
XLA Ops:
  0.6 0.0 copy-start
  0.6 54.9 %shard_map.41.x_ref = f32[10,512,128]{2,1,0:T(8,128)S(1)} custom-call(f32[1024,4096]{1,0:T(8,128)} %u_hbm.3), custom_call_target="tpu_custom_call" | custom-call | tf_op jit(solution)/shard_map/pallas_call | solution.py:410
  55.6 0.0 copy-done
  55.6 24.1 %shard_map.42 = (f32[1024,128]{1,0:T(8,128)}, f32[128,4096]{1,0:T(8,128)}) custom-call(f32[10,512,128]{2,1,0:T(8,128)S(1)} %shard_map.41.x_ref, f32[1024,128]{1,0:T(8,128)S(1)} %copy-done, f32[1024,4096]{1,0:T(8,128)} %u_hbm.3), custom_call_target="tpu_custom_call" | custom-call | tf_op jit(solution)/shard_map/pallas_call | solution.py:174
Async XLA Ops:
  0.6 54.9 %copy-start = (f32[1024,128]{1,0:T(8,128)S(1)}, f32[1024,128]{1,0:T(8,128)}, u32[]{:S(2)}) copy-start(f32[1024,128]{1,0:T(8,128)} %s_ref.1) | copy-start | bytes 1572868

commit v7 on v6

--- a/solution.py
+++ b/solution.py
@@ -186,7 +186,7 @@
 BLOCKS = [(i, j) for j in range(4) for i in range(j + 1)]
 STAGES = ((0, 3), (3, 6), (6, 8), (8, 10))
 KH = 2048
-ORDER = True
+
 LAT = (2.0, 3.9, 3.0)
 
 
@@ -394,7 +394,7 @@
     for _, s, ph in steps:
         left.setdefault(s, []).append(ph)
     while any(left.values()):
-        for s in sorted(left, reverse=ORDER):
+        for s in sorted(left, reverse=False):
             if left[s]:
                 red.step(s, left[s].pop(0))
     if comm:

time: 79.9 us -> 83 us (1.039)
  Pallas kernels: 79 us -> 82.1 us
    pallas_call x1, Pallas kernels: 54.9 us -> 58 us  [gram_reduce(): pl.pallas_call(functools.partial(gram_reduce_kernel, comm=comm), out_shap...]
where the time goes in v7:
time: 83 us; the launch traced here: 82.9 us
  Pallas kernels  82.1 us (99%)
    pallas_call x1, Pallas kernels, gram_reduce(): pl.pallas_call(functools.partial(gram_reduce_kernel, comm=comm), out_shap...  58 us
    pallas_call x1, Pallas kernels, iterate_project(): pl.pallas_call(tail_kernel, out_shape=(jax.ShapeDtypeStruct((1024, 128),...  24.1 us

profile of v7, /device:TPU:1, one launch (start us, length us, event | category | flops | bytes accessed | tf_op | source)
XLA Modules:
  0.0 82.9 jit_solution(17682983850321085261)
XLA Ops:
  0.6 0.0 copy-start
  0.6 58.0 %shard_map.41.x_ref = f32[10,512,128]{2,1,0:T(8,128)S(1)} custom-call(f32[1024,4096]{1,0:T(8,128)} %u_hbm.3), custom_call_target="tpu_custom_call" | custom-call | tf_op jit(solution)/shard_map/pallas_call | solution.py:410
  58.6 0.0 copy-done
  58.6 24.1 %shard_map.42 = (f32[1024,128]{1,0:T(8,128)}, f32[128,4096]{1,0:T(8,128)}) custom-call(f32[10,512,128]{2,1,0:T(8,128)S(1)} %shard_map.41.x_ref, f32[1024,128]{1,0:T(8,128)S(1)} %copy-done, f32[1024,4096]{1,0:T(8,128)} %u_hbm.3), custom_call_target="tpu_custom_call" | custom-call | tf_op jit(solution)/shard_map/pallas_call | solution.py:174
Async XLA Ops:
  0.6 58.0 %copy-start = (f32[1024,128]{1,0:T(8,128)S(1)}, f32[1024,128]{1,0:T(8,128)}, u32[]{:S(2)}) copy-start(f32[1024,128]{1,0:T(8,128)} %s_ref.1) | copy-start | bytes 1572868
